TPU v7x, 32 devices: a whole 2x2x4 slice. The times are simulated.
32 devices in a mesh: group: 2 (over y), gz: 4 (over z), gy: 2 (over x), gx: 2 (over core).
Axes of the slice: x: 2, y: 2, z: 4, core: 2. Of those that a mesh axis runs over, the one named last changes fastest.
Arguments:
- volume: bfloat16 [32, 32, 16, 512], P(None, ('group', 'gz'), 'gy', 'gx'), parts along dimension 1, may hold values from -6 to 6
- first_weight: bfloat16 [3, 3, 3, 32, 32], replicated, may hold values from -0.21875 to 0.21875
- second_weight: bfloat16 [3, 3, 3, 32, 32], replicated, may hold values from -0.21875 to 0.21875
- sample_index: int32 [8, 2, 2, 256], P(('group', 'gz'), 'gy', 'gx'), parts along dimension 0, may hold values from 0 to 8191
- segments: int32 [8, 2, 2, 256], P('group', 'gy', 'gx'), parts along dimension 0, may hold values from 0 to 63
- block_match: int32 [8, 4], P('group'), parts along dimension 0, may hold values from 0 to 1, as said below
Outputs:
- features: bfloat16 [32, 32, 16, 512], P(None, ('group', 'gz'), 'gy', 'gx'), parts along dimension 1
- row_loss: float32 [8, 2, 2, 256], P(('group', 'gz'), 'gy', 'gx'), parts along dimension 0
There are 2 independent parts, one for each index of `group`. A program takes and returns all parts, laid end to end along the dimension named above; an argument that names none is the same for every part. Nothing has to cross between parts.
Inputs may be any that keep to these rules, and one draw needn't show every extreme that they name: `sample_index`: the voxel of a row is z * 8 * 256 + y * 256 + x in its block's local coordinates. `block_match`: entry [a, a2] is 1 when block a contrasts against block a2; the diagonal is 1.
All inputs are finite; a program needn't handle non-finite values.
Results may differ from a plain program's by a relative error of at most 0.0034.
Values may be sent and summed in bfloat16 or wider, within the bound.
A program may use at most 128 MiB of HBM per device.

v0:
```python
import jax
import jax.numpy as jnp
from jax import lax
from jax.sharding import PartitionSpec as P

SOFTMAX_WARMTH = 0.25


def extended(shard, sides, width):
    for axis, dim in sides:
        count, length = (lax.axis_size(axis), shard.shape[dim])
        up = [(i, (i + 1) % count) for i in range(count - 1)]
        down = [(j, i) for i, j in up]
        last = lax.slice_in_dim(shard, length - width, length, axis=dim)
        leading = lax.slice_in_dim(shard, 0, width, axis=dim)
        before = lax.ppermute(last, axis, up)
        after = lax.ppermute(leading, axis, down)
        shard = jnp.concatenate([before, shard, after], axis=dim)
    return shard


def conv_valid(padded, weight):
    channels = padded.shape[0]
    out_z = padded.shape[1] - 2
    out_y = padded.shape[2] - 2
    out_x = padded.shape[3] - 2
    outputs = weight.shape[3]
    reduced_total = jnp.zeros((outputs, out_z * out_y * out_x), jnp.float32)
    for offset_z in range(3):
        plane = padded[:, offset_z : offset_z + out_z]
        stacked = jnp.stack(
            [
                plane[:, :, offset_y : offset_y + out_y, column_shift : column_shift + out_x]
                for offset_y in range(3)
                for column_shift in range(3)
            ],
            axis=0,
        )
        patches = stacked.reshape(9 * channels, out_z * out_y * out_x)
        kernel = jnp.transpose(weight[offset_z], (2, 0, 1, 3)).reshape(outputs, 9 * channels)
        reduced_total = reduced_total + jnp.dot(kernel, patches, preferred_element_type=jnp.float32)
    return reduced_total.reshape(outputs, out_z, out_y, out_x)


def pad_layer(activ_in):
    return extended(activ_in, (("gz", 1), ("gy", 2), ("gx", 3)), 1)


def shards(volume, first_weight, second_weight, sample_index, segments, block_match):
    channels, slab_depth, tile_height, tile_width = volume.shape
    hidden = jax.nn.relu(conv_valid(pad_layer(volume), first_weight)).astype(jnp.bfloat16)
    conv_out = conv_valid(pad_layer(hidden), second_weight)
    features = (conv_out + volume.astype(jnp.float32)).astype(jnp.bfloat16)
    flattened = features.reshape(channels, -1)
    picked = jnp.take(flattened, sample_index.reshape(-1), axis=1).astype(jnp.float32)
    embedding = (picked / jnp.sqrt(jnp.sum(picked * picked, axis=0) + 1.0)).astype(jnp.bfloat16)
    query_rows = embedding[None]
    own_block = lax.axis_index("gz")
    seg_all = segments.reshape(segments.shape[0], -1)
    home_segment_label = lax.dynamic_index_in_dim(seg_all, own_block, 0, keepdims=False)
    match_float = block_match.astype(jnp.float32)
    rows = embedding.shape[1]
    match_row = lax.dynamic_index_in_dim(match_float, own_block, 0, keepdims=False)
    similarity_logits = (
        jnp.einsum(
            "cr,kcs->rks",
            embedding,
            lax.all_gather(query_rows, "gz", axis=0, tiled=True),
            preferred_element_type=jnp.float32,
        )
        / SOFTMAX_WARMTH
    )
    same_seg = (home_segment_label[:, None, None] == seg_all[None]).astype(jnp.float32)
    exp_terms = jnp.exp(similarity_logits) * match_row[None, :, None]
    reduced_total = jnp.sum(exp_terms, axis=(1, 2))
    positive = jnp.sum(exp_terms * same_seg, axis=(1, 2))
    row_loss = (jnp.log(reduced_total) - jnp.log(positive)).reshape(1, 1, 1, rows)
    return (features, row_loss)


def solution(mesh):
    in_specs = (
        P(None, ("group", "gz"), "gy", "gx"),
        P(),
        P(),
        P(("group", "gz"), "gy", "gx", None),
        P("group", "gy", "gx", None),
        P("group", None),
    )
    out_specs = (P(None, ("group", "gz"), "gy", "gx"), P(("group", "gz"), "gy", "gx", None))
    return jax.shard_map(shards, mesh=mesh, in_specs=in_specs, out_specs=out_specs, check_vma=False)
```

profile of v0, /device:TPU:0, one launch (start us, length us, event | category | flops | bytes accessed | tf_op | source)
XLA Modules:
  0.0 274.9 jit_solution(13628984462543033317)
XLA Ops:
  1.6 4.9 %collective-permute-start = (bf16[32,1,8,256]{3,2,1,0:T(8,128)(2,1)S(1)}, bf16[32,1,8,256]{3,2,1,0:T(8,128)(2,1)S(1)}, u32[]{:S(2)}, u32[]{:S(2)}) collective-permute-start(bf16[32,1,8,256]{3,2,1,0:T(8,128)(2,1)S(1)} %get-tuple-element.74), channel_id=1, source_target_pairs={{0,4},{4,8},{8,12},{1,5},{5,9},{9,13},{2,6},{6,10},{10,14},{3,7},{... | collective-permute-start | bytes 393224 | tf_op jit(solution)/shard_map/ppermute | solution.py:16
  13.5 3.5 %copy.224 = bf16[32,6,8,256]{0,1,3,2:T(8,128)(2,1)} copy(bf16[32,6,8,256]{3,2,1,0:T(8,128)(2,1)S(1)} %constant_dynamic-update-slice_fusion) | data formatting | bytes 1572864 | tf_op jit(solution)/shard_map/concatenate | solution.py:18
  17.0 2.4 fusion.111
  19.4 3.4 %collective-permute-start.2 = (bf16[32,6,1,256]{0,1,3,2:T(8,128)(2,1)}, bf16[32,6,1,256]{0,1,3,2:T(8,128)(2,1)S(1)}, u32[]{:S(2)}, u32[]{:S(2)}) collective-permute-start(bf16[32,6,1,256]{0,1,3,2:T(8,128)(2,1)} %get-tuple-element.10), channel_id=1, source_target_pairs={{0,2},{1,3},{4,6},{5,7},{8,10},{9,11},{12,14},{13,15},{16,18},{17,... | collective-permute-start | bytes 294920 | tf_op jit(solution)/shard_map/ppermute | solution.py:16
  25.4 7.4 %collective-permute-done.2 = bf16[32,6,1,256]{0,1,3,2:T(8,128)(2,1)S(1)} collective-permute-done((bf16[32,6,1,256]{0,1,3,2:T(8,128)(2,1)}, bf16[32,6,1,256]{0,1,3,2:T(8,128)(2,1)S(1)}, u32[]{:S(2)}, u32[]{:S(2)}) %collective-permute-start.2) | collective-permute-done | bytes 98336 | tf_op jit(solution)/shard_map/ppermute | solution.py:16
  32.8 4.0 %collective-permute-done.3 = bf16[32,6,1,256]{0,1,3,2:T(8,128)(2,1)S(1)} collective-permute-done((bf16[32,6,1,256]{0,1,3,2:T(8,128)(2,1)}, bf16[32,6,1,256]{0,1,3,2:T(8,128)(2,1)S(1)}, u32[]{:S(2)}, u32[]{:S(2)}) %collective-permute-start.3) | collective-permute-done | bytes 98336 | tf_op jit(solution)/shard_map/ppermute | solution.py:17
  36.8 3.8 %pad_maximum_fusion = bf16[32,6,10,256]{0,1,3,2:T(8,128)(2,1)S(1)} fusion(bf16[32,6,1,256]{0,1,3,2:T(8,128)(2,1)S(1)} %collective-permute-done.3, bf16[32,6,8,256]{0,1,3,2:T(8,128)(2,1)} %copy.224, bf16[32,6,1,256]{0,1,3,2:T(8,128)(2,1)S(1)} %collective-permute-done.2), kind=kLoop, calls=%fused_computation.7 | loop fusion | flops 983040 | bytes 1966080 | tf_op jit(solution)/shard_map/concatenate | solution.py:18
  40.7 2.3 copy-done
  48.2 4.5 %copy.228 = bf16[32,6,10,256]{3,0,2,1:T(8,128)(2,1)S(1)} copy(bf16[32,6,10,256]{0,1,3,2:T(8,128)(2,1)} %copy-done) | data formatting | bytes 1966080 | tf_op jit(solution)/shard_map/concatenate | solution.py:18
  53.2 3.6 %fusion.94 = (bf16[1,32,4,8,256]{4,1,3,2,0:T(8,128)(2,1)}, bf16[1,32,4,8,256]{4,1,3,2,0:T(8,128)(2,1)S(1)}, bf16[1,32,4,8,256]{4,1,3,2,0:T(8,128)(2,1)}, bf16[1,...) fusion(bf16[32,6,10,256]{3,0,2,1:T(8,128)(2,1)S(1)} %copy.228, ...), kind=kLoop, calls=%fused_computation.193 | loop fusion | flops 9437184 | bytes 5705472 | tf_op jit(solution)/shard_map/stack | solution.py:31
  59.1 5.1 %fusion.92 = (bf16[1,32,4,8,256]{4,1,3,2,0:T(8,128)(2,1)S(1)}, bf16[1,32,4,8,256]{4,1,3,2,0:T(8,128)(2,1)S(1)}, bf16[1,32,4,8,256]{4,1,3,2,0:T(8,128)(2,1)S(1)},...) fusion(bf16[32,6,10,1]{3,0,2,1:T(8,128)(2,1)} %copy.232, ...), kind=kLoop, calls=%fused_computation.189 | loop fusion | flops 9437184 | bytes 5705472 | tf_op jit(solution)/shard_map/stack | solution.py:31
  84.5 8.4 %reshape.195 = bf16[288,8192]{1,0:T(8,128)(2,1)} reshape(bf16[9,32,4,8,256]{4,3,2,1,0:T(8,128)(2,1)} %copy_dynamic-update-slice_fusion.24) | data formatting | bytes 9437184 | tf_op jit(solution)/shard_map/reshape | solution.py:39
  96.1 8.8 %reshape.193 = bf16[288,8192]{1,0:T(8,128)(2,1)} reshape(bf16[9,32,4,8,256]{4,3,2,1,0:T(8,128)(2,1)} %copy_dynamic-update-slice_fusion.32) | data formatting | bytes 9437184 | tf_op jit(solution)/shard_map/reshape | solution.py:39
  109.3 8.3 %reshape.191 = bf16[288,8192]{1,0:T(8,128)(2,1)} reshape(bf16[9,32,4,8,256]{4,3,2,1,0:T(8,128)(2,1)} %copy_dynamic-update-slice_fusion.40) | data formatting | bytes 9437184 | tf_op jit(solution)/shard_map/reshape | solution.py:39
  117.6 3.5 %fusion.114 = f32[8192,32]{0,1:T(8,128)S(1)} fusion(bf16[32,288]{1,0:T(8,128)(2,1)S(1)} %reshape.192, bf16[288,8192]{1,0:T(8,128)(2,1)} %reshape.191), kind=kOutput, calls=%fused_computation.291 | convolution fusion | flops 150994944 | bytes 5785600 | tf_op jit(solution)/shard_map/dot_general | solution.py:41
  121.1 3.4 %convolution_add_fusion.3 = f32[8192,32]{0,1:T(8,128)S(1)} fusion(f32[8192,32]{0,1:T(8,128)S(1)} %fusion.114, bf16[32,288]{1,0:T(8,128)(2,1)S(1)} %reshape.194, bf16[288,8192]{1,0:T(8,128)(2,1)} %reshape.193), kind=kOutput, calls=%fused_computation.5 | convolution fusion | flops 151257088 | bytes 6834176 | tf_op jit(solution)/shard_map/dot_general | solution.py:41
  125.7 4.3 %collective-permute-start.6 = (bf16[32,1,8,256]{3,2,1,0:T(8,128)(2,1)S(1)}, bf16[32,1,8,256]{3,2,1,0:T(8,128)(2,1)S(1)}, u32[]{:S(2)}, u32[]{:S(2)}) collective-permute-start(bf16[32,1,8,256]{3,2,1,0:T(8,128)(2,1)S(1)} %get-tuple-element.69), channel_id=1, source_target_pairs={{0,4},{4,8},{8,12},{1,5},{5,9},{9,13},{2,6},{6,10},{10,14},{3,7},{... | collective-permute-start | bytes 393224 | tf_op jit(solution)/shard_map/ppermute | solution.py:16
  133.8 6.7 %collective-permute-done.7 = bf16[32,1,8,256]{3,2,1,0:T(8,128)(2,1)S(1)} collective-permute-done((bf16[32,1,8,256]{3,2,1,0:T(8,128)(2,1)S(1)}, bf16[32,1,8,256]{3,2,1,0:T(8,128)(2,1)S(1)}, u32[]{:S(2)}, u32[]{:S(2)}) %collective-permute-start.7) | collective-permute-done | bytes 131104 | tf_op jit(solution)/shard_map/ppermute | solution.py:17
  140.5 3.5 %copy.262 = bf16[32,6,8,256]{0,1,3,2:T(8,128)(2,1)} copy(bf16[32,6,8,256]{3,2,1,0:T(8,128)(2,1)S(1)} %constant_dynamic-update-slice_fusion.3) | data formatting | bytes 1572864 | tf_op jit(solution)/shard_map/concatenate | solution.py:18
  149.1 9.1 %collective-permute-done.8 = bf16[32,6,1,256]{0,1,3,2:T(8,128)(2,1)S(1)} collective-permute-done((bf16[32,6,1,256]{0,1,3,2:T(8,128)(2,1)S(1)}, bf16[32,6,1,256]{0,1,3,2:T(8,128)(2,1)S(1)}, u32[]{:S(2)}, u32[]{:S(2)}) %collective-permute-start.8) | collective-permute-done | bytes 98336 | tf_op jit(solution)/shard_map/ppermute | solution.py:16
  158.3 4.1 %collective-permute-done.9 = bf16[32,6,1,256]{0,1,3,2:T(8,128)(2,1)S(1)} collective-permute-done((bf16[32,6,1,256]{0,1,3,2:T(8,128)(2,1)S(1)}, bf16[32,6,1,256]{0,1,3,2:T(8,128)(2,1)S(1)}, u32[]{:S(2)}, u32[]{:S(2)}) %collective-permute-start.9) | collective-permute-done | bytes 98336 | tf_op jit(solution)/shard_map/ppermute | solution.py:17
  162.4 4.0 %pad_maximum_fusion.1 = bf16[32,6,10,256]{0,1,3,2:T(8,128)(2,1)S(1)} fusion(bf16[32,6,1,256]{0,1,3,2:T(8,128)(2,1)S(1)} %collective-permute-done.9, bf16[32,6,8,256]{0,1,3,2:T(8,128)(2,1)} %copy.262, bf16[32,6,1,256]{0,1,3,2:T(8,128)(2,1)S(1)} %collective-permute-done.8), kind=kLoop, calls=%fused_computation.8 | loop fusion | flops 983040 | bytes 1966080 | tf_op jit(solution)/shard_map/concatenate | solution.py:18
  166.5 2.3 copy-done.1
  175.4 4.7 %copy.266 = bf16[32,6,10,256]{3,0,2,1:T(8,128)(2,1)S(1)} copy(bf16[32,6,10,256]{0,1,3,2:T(8,128)(2,1)} %copy-done.1) | data formatting | bytes 1966080 | tf_op jit(solution)/shard_map/concatenate | solution.py:18
  180.5 3.7 %fusion.86 = (bf16[1,32,4,8,256]{4,1,3,2,0:T(8,128)(2,1)}, bf16[1,32,4,8,256]{4,1,3,2,0:T(8,128)(2,1)S(1)}, bf16[1,32,4,8,256]{4,1,3,2,0:T(8,128)(2,1)}, bf16[1,...) fusion(bf16[32,6,10,256]{3,0,2,1:T(8,128)(2,1)S(1)} %copy.266, ...), kind=kLoop, calls=%fused_computation.179 | loop fusion | flops 9437184 | bytes 5705472 | tf_op jit(solution)/shard_map/stack | solution.py:31
  186.5 5.4 %fusion.84 = (bf16[1,32,4,8,256]{4,1,3,2,0:T(8,128)(2,1)S(1)}, bf16[1,32,4,8,256]{4,1,3,2,0:T(8,128)(2,1)S(1)}, bf16[1,32,4,8,256]{4,1,3,2,0:T(8,128)(2,1)}, bf1...) fusion(bf16[32,6,10,1]{3,0,2,1:T(8,128)(2,1)} %copy.270, ...), kind=kLoop, calls=%fused_computation.175 | loop fusion | flops 9437184 | bytes 5705472 | tf_op jit(solution)/shard_map/stack | solution.py:31
  206.2 8.3 %reshape.201 = bf16[288,8192]{1,0:T(8,128)(2,1)} reshape(bf16[9,32,4,8,256]{4,3,2,1,0:T(8,128)(2,1)} %copy_dynamic-update-slice_fusion) | data formatting | bytes 9437184 | tf_op jit(solution)/shard_map/reshape | solution.py:39
  228.4 8.5 %reshape.199 = bf16[288,8192]{1,0:T(8,128)(2,1)} reshape(bf16[9,32,4,8,256]{4,3,2,1,0:T(8,128)(2,1)} %copy_dynamic-update-slice_fusion.8) | data formatting | bytes 9437184 | tf_op jit(solution)/shard_map/reshape | solution.py:39
  241.3 8.3 %reshape.197 = bf16[288,8192]{1,0:T(8,128)(2,1)} reshape(bf16[9,32,4,8,256]{4,3,2,1,0:T(8,128)(2,1)} %copy_dynamic-update-slice_fusion.16) | data formatting | bytes 9437184 | tf_op jit(solution)/shard_map/reshape | solution.py:39
  249.6 3.5 %fusion.115 = f32[8192,32]{0,1:T(8,128)S(1)} fusion(bf16[32,288]{1,0:T(8,128)(2,1)S(1)} %copy-done.32, bf16[288,8192]{1,0:T(8,128)(2,1)} %reshape.197), kind=kOutput, calls=%fused_computation.292 | convolution fusion | flops 150994944 | bytes 5785600 | tf_op jit(solution)/shard_map/dot_general | solution.py:41
  253.1 3.4 %convolution_add_fusion.1 = f32[8192,32]{0,1:T(8,128)S(1)} fusion(f32[8192,32]{0,1:T(8,128)S(1)} %fusion.115, bf16[32,288]{1,0:T(8,128)(2,1)S(1)} %copy-done.33, bf16[288,8192]{1,0:T(8,128)(2,1)} %reshape.199), kind=kOutput, calls=%fused_computation.2 | convolution fusion | flops 151257088 | bytes 6834176 | tf_op jit(solution)/shard_map/dot_general | solution.py:41
  260.2 13.4 %all_gather.3 = bf16[4,32,256]{2,1,0:T(8,128)(2,1)S(1)} all-gather(bf16[1,32,256]{2,1,0:T(8,128)(2,1)S(1)} %divide_convert_fusion), channel_id=1, replica_groups=mesh['group'=2,'gz'=4,'gy'=2,'gx'=2] {'gz'}, dimensions={0}, use_global_device_ids=true | all-gather | bytes 81920 | tf_op jit(solution)/shard_map/all_gather | solution.py:68
  (211 shorter events, 102.6 us)
Async XLA Ops:
  1.6 9.6 %collective-permute-start = (bf16[32,1,8,256]{3,2,1,0:T(8,128)(2,1)S(1)}, bf16[32,1,8,256]{3,2,1,0:T(8,128)(2,1)S(1)}, u32[]{:S(2)}, u32[]{:S(2)}) collective-permute-start(bf16[32,1,8,256]{3,2,1,0:T(8,128)(2,1)S(1)} %get-tuple-element.74), channel_id=1, source_target_pairs={{0,4},{4,8},{8,12},{1,5},{5,9},{9,13},{2,6},{6,10},{10,14},{3,7},{... | collective-permute-start | bytes 393224 | tf_op jit(solution)/shard_map/ppermute | solution.py:16
  6.6 17.5 %copy-start.37 = (s32[1,1,1,256]{3,2,1,0:T(1,128)S(1)}, s32[1,1,1,256]{3,2,1,0:T(1,128)}, u32[]{:S(2)}) copy-start(s32[1,1,1,256]{3,2,1,0:T(1,128)} %param.9) | copy-start | bytes 3076
  6.6 6.9 %collective-permute-start.1 = (bf16[32,1,8,256]{3,2,1,0:T(8,128)(2,1)S(1)}, bf16[32,1,8,256]{3,2,1,0:T(8,128)(2,1)S(1)}, u32[]{:S(2)}, u32[]{:S(2)}) collective-permute-start(bf16[32,1,8,256]{3,2,1,0:T(8,128)(2,1)S(1)} %get-tuple-element.73), channel_id=1, source_target_pairs={{4,0},{8,4},{12,8},{5,1},{9,5},{13,9},{6,2},{10,6},{14,10},{7,3},{... | collective-permute-start | bytes 393224 | tf_op jit(solution)/shard_map/ppermute | solution.py:17
  19.4 13.5 %collective-permute-start.2 = (bf16[32,6,1,256]{0,1,3,2:T(8,128)(2,1)}, bf16[32,6,1,256]{0,1,3,2:T(8,128)(2,1)S(1)}, u32[]{:S(2)}, u32[]{:S(2)}) collective-permute-start(bf16[32,6,1,256]{0,1,3,2:T(8,128)(2,1)} %get-tuple-element.10), channel_id=1, source_target_pairs={{0,2},{1,3},{4,6},{5,7},{8,10},{9,11},{12,14},{13,15},{16,18},{17,... | collective-permute-start | bytes 294920 | tf_op jit(solution)/shard_map/ppermute | solution.py:16
  22.8 14.1 %collective-permute-start.3 = (bf16[32,6,1,256]{0,1,3,2:T(8,128)(2,1)}, bf16[32,6,1,256]{0,1,3,2:T(8,128)(2,1)S(1)}, u32[]{:S(2)}, u32[]{:S(2)}) collective-permute-start(bf16[32,6,1,256]{0,1,3,2:T(8,128)(2,1)} %get-tuple-element.11), channel_id=1, source_target_pairs={{2,0},{3,1},{6,4},{7,5},{10,8},{11,9},{14,12},{15,13},{18,16},{19,... | collective-permute-start | bytes 294920 | tf_op jit(solution)/shard_map/ppermute | solution.py:17
  43.0 9.7 %collective-permute-start.4 = (bf16[32,6,10,1]{0,1,3,2:T(8,128)(2,1)S(1)}, bf16[32,6,10,1]{0,1,3,2:T(8,128)(2,1)S(1)}, u32[]{:S(2)}, u32[]{:S(2)}) collective-permute-start(bf16[32,6,10,1]{0,1,3,2:T(8,128)(2,1)S(1)} %get-tuple-element.7), channel_id=1, source_target_pairs={{0,1},{2,3},{4,5},{6,7},{8,9},{10,11},{12,13},{14,15},{16,17},{18,... | collective-permute-start | bytes 11528 | tf_op jit(solution)/shard_map/ppermute | solution.py:16
  44.3 13.5 %collective-permute-start.5 = (bf16[32,6,10,1]{0,1,3,2:T(8,128)(2,1)S(1)}, bf16[32,6,10,1]{0,1,3,2:T(8,128)(2,1)S(1)}, u32[]{:S(2)}, u32[]{:S(2)}) collective-permute-start(bf16[32,6,10,1]{0,1,3,2:T(8,128)(2,1)S(1)} %get-tuple-element.6), channel_id=1, source_target_pairs={{1,0},{3,2},{5,4},{7,6},{9,8},{11,10},{13,12},{15,14},{17,16},{19,... | collective-permute-start | bytes 11528 | tf_op jit(solution)/shard_map/ppermute | solution.py:17
  59.1 10.6 %copy-start.12 = (bf16[1,32,4,8,256]{4,1,3,2,0:T(8,128)(2,1)S(1)}, bf16[1,32,4,8,256]{4,1,3,2,0:T(8,128)(2,1)}, u32[]{:S(2)}) copy-start(bf16[1,32,4,8,256]{4,1,3,2,0:T(8,128)(2,1)} %get-tuple-element.41) | copy-start | bytes 1572868
  59.1 11.7 %copy-start.26 = (bf16[1,32,4,8,256]{4,1,3,2,0:T(8,128)(2,1)S(1)}, bf16[1,32,4,8,256]{4,1,3,2,0:T(8,128)(2,1)}, u32[]{:S(2)}) copy-start(bf16[1,32,4,8,256]{4,1,3,2,0:T(8,128)(2,1)} %get-tuple-element.63) | copy-start | bytes 1572868
  64.2 9.8 %copy-start.25 = (bf16[1,32,4,8,256]{4,1,3,2,0:T(8,128)(2,1)S(1)}, bf16[1,32,4,8,256]{4,1,3,2,0:T(8,128)(2,1)}, u32[]{:S(2)}) copy-start(bf16[1,32,4,8,256]{4,1,3,2,0:T(8,128)(2,1)} %get-tuple-element.65) | copy-start | bytes 1572868
  65.3 10.9 %copy-start.9 = (bf16[1,32,4,8,256]{4,1,3,2,0:T(8,128)(2,1)S(1)}, bf16[1,32,4,8,256]{4,1,3,2,0:T(8,128)(2,1)}, u32[]{:S(2)}) copy-start(bf16[1,32,4,8,256]{4,1,3,2,0:T(8,128)(2,1)} %get-tuple-element.47) | copy-start | bytes 1572868
  66.4 10.9 %copy-start.2 = (bf16[32,4,8,256]{3,2,1,0:T(8,128)(2,1)S(1)}, bf16[32,4,8,256]{3,2,1,0:T(8,128)(2,1)}, u32[]{:S(2)}) copy-start(bf16[32,4,8,256]{3,2,1,0:T(8,128)(2,1)} %param.6) | copy-start | bytes 1572868
  84.5 10.5 %copy-start.5 = (bf16[1,32,4,8,256]{4,1,3,2,0:T(8,128)(2,1)S(1)}, bf16[1,32,4,8,256]{4,1,3,2,0:T(8,128)(2,1)}, u32[]{:S(2)}) copy-start(bf16[1,32,4,8,256]{4,1,3,2,0:T(8,128)(2,1)} %get-tuple-element.36) | copy-start | bytes 1572868
  96.1 11.0 %copy-start.20 = (bf16[1,32,4,8,256]{4,1,3,2,0:T(8,128)(2,1)S(1)}, bf16[1,32,4,8,256]{4,1,3,2,0:T(8,128)(2,1)}, u32[]{:S(2)}) copy-start(bf16[1,32,4,8,256]{4,1,3,2,0:T(8,128)(2,1)} %get-tuple-element.55) | copy-start | bytes 1572868
  125.7 8.0 %collective-permute-start.6 = (bf16[32,1,8,256]{3,2,1,0:T(8,128)(2,1)S(1)}, bf16[32,1,8,256]{3,2,1,0:T(8,128)(2,1)S(1)}, u32[]{:S(2)}, u32[]{:S(2)}) collective-permute-start(bf16[32,1,8,256]{3,2,1,0:T(8,128)(2,1)S(1)} %get-tuple-element.69), channel_id=1, source_target_pairs={{0,4},{4,8},{8,12},{1,5},{5,9},{9,13},{2,6},{6,10},{10,14},{3,7},{... | collective-permute-start | bytes 393224 | tf_op jit(solution)/shard_map/ppermute | solution.py:16
  132.3 8.1 %collective-permute-start.7 = (bf16[32,1,8,256]{3,2,1,0:T(8,128)(2,1)S(1)}, bf16[32,1,8,256]{3,2,1,0:T(8,128)(2,1)S(1)}, u32[]{:S(2)}, u32[]{:S(2)}) collective-permute-start(bf16[32,1,8,256]{3,2,1,0:T(8,128)(2,1)S(1)} %get-tuple-element.68), channel_id=1, source_target_pairs={{4,0},{8,4},{12,8},{5,1},{9,5},{13,9},{6,2},{10,6},{14,10},{7,3},{... | collective-permute-start | bytes 393224 | tf_op jit(solution)/shard_map/ppermute | solution.py:17
  140.5 26.0 %copy-start.28 = (bf16[32,1,8,256]{3,2,1,0:T(8,128)(2,1)}, bf16[32,1,8,256]{3,2,1,0:T(8,128)(2,1)S(1)}, u32[]{:S(2)}) copy-start(bf16[32,1,8,256]{3,2,1,0:T(8,128)(2,1)S(1)} %collective-permute-done.7) | copy-start | bytes 393220
  145.4 12.9 %collective-permute-start.8 = (bf16[32,6,1,256]{0,1,3,2:T(8,128)(2,1)S(1)}, bf16[32,6,1,256]{0,1,3,2:T(8,128)(2,1)S(1)}, u32[]{:S(2)}, u32[]{:S(2)}) collective-permute-start(bf16[32,6,1,256]{0,1,3,2:T(8,128)(2,1)S(1)} %get-tuple-element.8), channel_id=1, source_target_pairs={{0,2},{1,3},{4,6},{5,7},{8,10},{9,11},{12,14},{13,15},{16,18},{17,... | collective-permute-start | bytes 294920 | tf_op jit(solution)/shard_map/ppermute | solution.py:16
  147.0 15.4 %collective-permute-start.9 = (bf16[32,6,1,256]{0,1,3,2:T(8,128)(2,1)S(1)}, bf16[32,6,1,256]{0,1,3,2:T(8,128)(2,1)S(1)}, u32[]{:S(2)}, u32[]{:S(2)}) collective-permute-start(bf16[32,6,1,256]{0,1,3,2:T(8,128)(2,1)S(1)} %get-tuple-element.9), channel_id=1, source_target_pairs={{2,0},{3,1},{6,4},{7,5},{10,8},{11,9},{14,12},{15,13},{18,16},{19,... | collective-permute-start | bytes 294920 | tf_op jit(solution)/shard_map/ppermute | solution.py:17
  169.5 10.6 %collective-permute-start.10 = (bf16[32,6,10,1]{0,1,3,2:T(8,128)(2,1)}, bf16[32,6,10,1]{0,1,3,2:T(8,128)(2,1)S(1)}, u32[]{:S(2)}, u32[]{:S(2)}) collective-permute-start(bf16[32,6,10,1]{0,1,3,2:T(8,128)(2,1)} %get-tuple-element.5), channel_id=1, source_target_pairs={{0,1},{2,3},{4,5},{6,7},{8,9},{10,11},{12,13},{14,15},{16,17},{18,... | collective-permute-start | bytes 11528 | tf_op jit(solution)/shard_map/ppermute | solution.py:16
  170.7 14.6 %collective-permute-start.11 = (bf16[32,6,10,1]{0,1,3,2:T(8,128)(2,1)}, bf16[32,6,10,1]{0,1,3,2:T(8,128)(2,1)S(1)}, u32[]{:S(2)}, u32[]{:S(2)}) collective-permute-start(bf16[32,6,10,1]{0,1,3,2:T(8,128)(2,1)} %get-tuple-element.4), channel_id=1, source_target_pairs={{1,0},{3,2},{5,4},{7,6},{9,8},{11,10},{13,12},{15,14},{17,16},{19,... | collective-permute-start | bytes 11528 | tf_op jit(solution)/shard_map/ppermute | solution.py:17
  186.5 9.8 %copy-start.13 = (bf16[1,32,4,8,256]{4,1,3,2,0:T(8,128)(2,1)S(1)}, bf16[1,32,4,8,256]{4,1,3,2,0:T(8,128)(2,1)}, u32[]{:S(2)}) copy-start(bf16[1,32,4,8,256]{4,1,3,2,0:T(8,128)(2,1)} %get-tuple-element.23) | copy-start | bytes 1572868
  186.5 10.9 %copy-start.27 = (bf16[1,32,4,8,256]{4,1,3,2,0:T(8,128)(2,1)S(1)}, bf16[1,32,4,8,256]{4,1,3,2,0:T(8,128)(2,1)}, u32[]{:S(2)}) copy-start(bf16[1,32,4,8,256]{4,1,3,2,0:T(8,128)(2,1)} %get-tuple-element.62) | copy-start | bytes 1572868
  186.5 13.1 %copy-start.11 = (bf16[1,32,4,8,256]{4,1,3,2,0:T(8,128)(2,1)S(1)}, bf16[1,32,4,8,256]{4,1,3,2,0:T(8,128)(2,1)}, u32[]{:S(2)}) copy-start(bf16[1,32,4,8,256]{4,1,3,2,0:T(8,128)(2,1)} %get-tuple-element.29) | copy-start | bytes 1572868
  193.1 9.9 %copy-start.8 = (bf16[1,32,4,8,256]{4,1,3,2,0:T(8,128)(2,1)S(1)}, bf16[1,32,4,8,256]{4,1,3,2,0:T(8,128)(2,1)}, u32[]{:S(2)}) copy-start(bf16[1,32,4,8,256]{4,1,3,2,0:T(8,128)(2,1)} %get-tuple-element.21) | copy-start | bytes 1572868
  214.5 10.6 %copy-start.3 = (bf16[1,32,4,8,256]{4,1,3,2,0:T(8,128)(2,1)S(1)}, bf16[1,32,4,8,256]{4,1,3,2,0:T(8,128)(2,1)}, u32[]{:S(2)}) copy-start(bf16[1,32,4,8,256]{4,1,3,2,0:T(8,128)(2,1)} %get-tuple-element.27) | copy-start | bytes 1572868
  214.5 11.7 %copy-start.22 = (bf16[1,32,4,8,256]{4,1,3,2,0:T(8,128)(2,1)S(1)}, bf16[1,32,4,8,256]{4,1,3,2,0:T(8,128)(2,1)}, u32[]{:S(2)}) copy-start(bf16[1,32,4,8,256]{4,1,3,2,0:T(8,128)(2,1)} %get-tuple-element.50) | copy-start | bytes 1572868
  214.5 12.8 %copy-start.6 = (bf16[1,32,4,8,256]{4,1,3,2,0:T(8,128)(2,1)S(1)}, bf16[1,32,4,8,256]{4,1,3,2,0:T(8,128)(2,1)}, u32[]{:S(2)}) copy-start(bf16[1,32,4,8,256]{4,1,3,2,0:T(8,128)(2,1)} %get-tuple-element.18) | copy-start | bytes 1572868
  228.4 10.8 %copy-start.21 = (bf16[1,32,4,8,256]{4,1,3,2,0:T(8,128)(2,1)S(1)}, bf16[1,32,4,8,256]{4,1,3,2,0:T(8,128)(2,1)}, u32[]{:S(2)}) copy-start(bf16[1,32,4,8,256]{4,1,3,2,0:T(8,128)(2,1)} %get-tuple-element.49) | copy-start | bytes 1572868
  257.6 16.0 %copy-start.38 = (s32[1,1,1,256]{3,2,1,0:T(1,128)S(1)}, s32[1,1,1,256]{3,2,1,0:T(1,128)}, u32[]{:S(2)}) copy-start(s32[1,1,1,256]{3,2,1,0:T(1,128)} %constant_dynamic-slice_fusion) | copy-start | bytes 3076
  257.6 16.0 %copy-start.39 = (f32[4]{0:T(128)S(1)}, f32[4]{0:T(128)}, u32[]{:S(2)}) copy-start(f32[4]{0:T(128)} %dynamic-slice_bitcast_fusion) | copy-start | bytes 52
  258.1 16.6 %copy-start.19 = (bf16[32,4,8,256]{3,2,1,0:T(8,128)(2,1)}, bf16[32,4,8,256]{3,2,1,0:T(8,128)(2,1)S(1)}, u32[]{:S(2)}) copy-start(bf16[32,4,8,256]{3,2,1,0:T(8,128)(2,1)S(1)} %add_convert_fusion) | copy-start | bytes 1572868
  (24 other events, 151.0 us)
where the time goes:
time: 280 us; the launch traced here: 275 us
  local copies, waits for them, and re-layouts  153 us (55%)
  other arithmetic  33.5 us (12%)
  waiting for transfers between devices  32.7 us (12%)
  starting transfers between devices  24.8 us (9%)
  matrix products  16.3 us (6%)
  blocking collectives  13.4 us (5%)
    unnamed x137, local copies, waits for them, and re-layouts  59.9 us
    reshape x6, local copies, waits for them, and re-layouts, conv_valid(): patches = stacked.reshape(9 * channels, out_z * out_y * out_x)  50.6 us
    another operation x6, other arithmetic, conv_valid(): jnp.stack([plane[:, :, offset_y:offset_y + out_y, column_shift:column_shi...  21.2 us
    concatenate x8, local copies, waits for them, and re-layouts, extended(): shard = jnp.concatenate([before, shard, after], axis=dim)  16.8 us
    ppermute x6, starting transfers between devices, extended(): before = lax.ppermute(last, axis, up)  16.8 us
    ppermute x6, waiting for transfers between devices, extended(): before = lax.ppermute(last, axis, up)  16.6 us
    ppermute x6, waiting for transfers between devices, extended(): after = lax.ppermute(leading, axis, down)  16 us
    dot_general x6, matrix products, conv_valid(): jnp.dot(kernel, patches, preferred_element_type=jnp.float32)  15.8 us
  transfers between devices with their start and end apart: 12, of which 7 were waited for; matrix products, arithmetic and copies ran while one was open for 12% of the time, Pallas kernels for 0%

commit v1 on v0

--- a/solution.py
+++ b/solution.py
@@ -4,6 +4,21 @@
 from jax.sharding import PartitionSpec as P
 
 SOFTMAX_WARMTH = 0.25
+
+
+def work_around(x, axis, dim, make, out_dim):
+    ways, here, step = (lax.axis_size(axis), lax.axis_index(axis), x.shape[dim])
+    results = []
+    for far in range(ways):
+        arriving = (
+            lax.ppermute(x, axis, [(d, (d + 1) % ways) for d in range(ways)])
+            if far + 1 < ways
+            else x
+        )
+        results.append(make(x, (here - far) % ways * step))
+        x = arriving
+    line = jnp.concatenate(results[::-1], axis=out_dim)
+    return jnp.roll(line, (here + 1) * results[0].shape[out_dim], axis=out_dim)
 
 
 def extended(shard, sides, width):
@@ -62,11 +77,14 @@
     rows = embedding.shape[1]
     match_row = lax.dynamic_index_in_dim(match_float, own_block, 0, keepdims=False)
     similarity_logits = (
-        jnp.einsum(
-            "cr,kcs->rks",
-            embedding,
-            lax.all_gather(query_rows, "gz", axis=0, tiled=True),
-            preferred_element_type=jnp.float32,
+        work_around(
+            query_rows,
+            "gz",
+            0,
+            lambda shard_2, offset: jnp.einsum(
+                "cr,kcs->rks", embedding, shard_2, preferred_element_type=jnp.float32
+            ),
+            1,
         )
         / SOFTMAX_WARMTH
     )

time: 280 us -> 287 us (1.025)
  waiting for transfers between devices: 32.7 us -> 51.4 us
  blocking collectives: 13.4 us -> 0 us
    ppermute x0 -> x3, waiting for transfers between devices: none -> 16.8 us  [work_around(): lax.ppermute(x, axis, [(d, (d + 1) % ways) for d in range(ways)])]
    all_gather x1 -> x0, blocking collectives: 13.4 us -> none  [shards(): lax.all_gather(query_rows, 'gz', axis=0, tiled=True)]
    unnamed x137 -> x128, local copies, waits for them, and re-layouts: 59.9 us -> 60.3 us
  transfers between devices with their start and end apart: 12 -> 15, of which waited for: 7 -> 10; matrix products, arithmetic and copies ran while one was open for 12% -> 11% of each run, Pallas kernels for 0% -> 0%
where the time goes in v1:
time: 287 us; the launch traced here: 281 us
  local copies, waits for them, and re-layouts  152 us (53%)
  waiting for transfers between devices  51.4 us (18%)
  other arithmetic  33.4 us (12%)
  starting transfers between devices  26.2 us (9%)
  matrix products  17 us (6%)
    unnamed x128, local copies, waits for them, and re-layouts  60.3 us
    reshape x6, local copies, waits for them, and re-layouts, conv_valid(): patches = stacked.reshape(9 * channels, out_z * out_y * out_x)  50.6 us
    another operation x6, other arithmetic, conv_valid(): jnp.stack([plane[:, :, offset_y:offset_y + out_y, column_shift:column_shi...  21.3 us
    ppermute x6, waiting for transfers between devices, extended(): before = lax.ppermute(last, axis, up)  19 us
    ppermute x3, waiting for transfers between devices, work_around(): lax.ppermute(x, axis, [(d, (d + 1) % ways) for d in range(ways)])  16.8 us
    concatenate x8, local copies, waits for them, and re-layouts, extended(): shard = jnp.concatenate([before, shard, after], axis=dim)  16.8 us
    ppermute x6, starting transfers between devices, extended(): before = lax.ppermute(last, axis, up)  16.6 us
    dot_general x6, matrix products, conv_valid(): jnp.dot(kernel, patches, preferred_element_type=jnp.float32)  15.8 us
  transfers between devices with their start and end apart: 15, of which 10 were waited for; matrix products, arithmetic and copies ran while one was open for 11% of the time, Pallas kernels for 0%

profile of v1, /device:TPU:0, one launch (start us, length us, event | category | flops | bytes accessed | tf_op | source)
XLA Modules:
  0.0 281.2 jit_solution(10569204852346299382)
XLA Ops:
  1.6 4.9 %collective-permute-start = (bf16[32,1,8,256]{3,2,1,0:T(8,128)(2,1)S(1)}, bf16[32,1,8,256]{3,2,1,0:T(8,128)(2,1)S(1)}, u32[]{:S(2)}, u32[]{:S(2)}) collective-permute-start(bf16[32,1,8,256]{3,2,1,0:T(8,128)(2,1)S(1)} %get-tuple-element.74), channel_id=1, source_target_pairs={{0,4},{4,8},{8,12},{1,5},{5,9},{9,13},{2,6},{6,10},{10,14},{3,7},{... | collective-permute-start | bytes 393224 | tf_op jit(solution)/shard_map/ppermute | solution.py:31
  10.9 2.5 collective-permute-done.1
  13.5 3.5 %copy.137 = bf16[32,6,8,256]{0,1,3,2:T(8,128)(2,1)} copy(bf16[32,6,8,256]{3,2,1,0:T(8,128)(2,1)S(1)} %constant_dynamic-update-slice_fusion) | data formatting | bytes 1572864 | tf_op jit(solution)/shard_map/concatenate | solution.py:33
  19.3 3.4 %collective-permute-start.2 = (bf16[32,6,1,256]{0,1,3,2:T(8,128)(2,1)}, bf16[32,6,1,256]{0,1,3,2:T(8,128)(2,1)S(1)}, u32[]{:S(2)}, u32[]{:S(2)}) collective-permute-start(bf16[32,6,1,256]{0,1,3,2:T(8,128)(2,1)} %get-tuple-element.10), channel_id=1, source_target_pairs={{0,2},{1,3},{4,6},{5,7},{8,10},{9,11},{12,14},{13,15},{16,18},{17,... | collective-permute-start | bytes 294920 | tf_op jit(solution)/shard_map/ppermute | solution.py:31
  25.4 7.4 %collective-permute-done.2 = bf16[32,6,1,256]{0,1,3,2:T(8,128)(2,1)S(1)} collective-permute-done((bf16[32,6,1,256]{0,1,3,2:T(8,128)(2,1)}, bf16[32,6,1,256]{0,1,3,2:T(8,128)(2,1)S(1)}, u32[]{:S(2)}, u32[]{:S(2)}) %collective-permute-start.2) | collective-permute-done | bytes 98336 | tf_op jit(solution)/shard_map/ppermute | solution.py:31
  32.8 4.0 %collective-permute-done.3 = bf16[32,6,1,256]{0,1,3,2:T(8,128)(2,1)S(1)} collective-permute-done((bf16[32,6,1,256]{0,1,3,2:T(8,128)(2,1)}, bf16[32,6,1,256]{0,1,3,2:T(8,128)(2,1)S(1)}, u32[]{:S(2)}, u32[]{:S(2)}) %collective-permute-start.3) | collective-permute-done | bytes 98336 | tf_op jit(solution)/shard_map/ppermute | solution.py:32
  36.8 3.8 %pad_maximum_fusion = bf16[32,6,10,256]{0,1,3,2:T(8,128)(2,1)S(1)} fusion(bf16[32,6,1,256]{0,1,3,2:T(8,128)(2,1)S(1)} %collective-permute-done.3, bf16[32,6,8,256]{0,1,3,2:T(8,128)(2,1)} %copy.137, bf16[32,6,1,256]{0,1,3,2:T(8,128)(2,1)S(1)} %collective-permute-done.2), kind=kLoop, calls=%fused_computation.7 | loop fusion | flops 983040 | bytes 1966080 | tf_op jit(solution)/shard_map/concatenate | solution.py:33
  48.2 4.5 %copy.141 = bf16[32,6,10,256]{3,0,2,1:T(8,128)(2,1)S(1)} copy(bf16[32,6,10,256]{0,1,3,2:T(8,128)(2,1)} %copy-done) | data formatting | bytes 1966080 | tf_op jit(solution)/shard_map/concatenate | solution.py:33
  53.2 3.6 %fusion.93 = (bf16[1,32,4,8,256]{4,1,3,2,0:T(8,128)(2,1)}, bf16[1,32,4,8,256]{4,1,3,2,0:T(8,128)(2,1)S(1)}, bf16[1,32,4,8,256]{4,1,3,2,0:T(8,128)(2,1)}, bf16[1,...) fusion(bf16[32,6,10,256]{3,0,2,1:T(8,128)(2,1)S(1)} %copy.141, ...), kind=kLoop, calls=%fused_computation.196 | loop fusion | flops 9437184 | bytes 5705472 | tf_op jit(solution)/shard_map/stack | solution.py:46
  59.1 5.1 %fusion.91 = (bf16[1,32,4,8,256]{4,1,3,2,0:T(8,128)(2,1)S(1)}, bf16[1,32,4,8,256]{4,1,3,2,0:T(8,128)(2,1)S(1)}, bf16[1,32,4,8,256]{4,1,3,2,0:T(8,128)(2,1)S(1)},...) fusion(bf16[32,6,10,1]{3,0,2,1:T(8,128)(2,1)} %copy.145, ...), kind=kLoop, calls=%fused_computation.192 | loop fusion | flops 9437184 | bytes 5705472 | tf_op jit(solution)/shard_map/stack | solution.py:46
  84.6 8.4 %reshape.217 = bf16[288,8192]{1,0:T(8,128)(2,1)} reshape(bf16[9,32,4,8,256]{4,3,2,1,0:T(8,128)(2,1)} %copy_dynamic-update-slice_fusion.24) | data formatting | bytes 9437184 | tf_op jit(solution)/shard_map/reshape | solution.py:54
  96.2 8.8 %reshape.215 = bf16[288,8192]{1,0:T(8,128)(2,1)} reshape(bf16[9,32,4,8,256]{4,3,2,1,0:T(8,128)(2,1)} %copy_dynamic-update-slice_fusion.32) | data formatting | bytes 9437184 | tf_op jit(solution)/shard_map/reshape | solution.py:54
  109.4 8.3 %reshape.213 = bf16[288,8192]{1,0:T(8,128)(2,1)} reshape(bf16[9,32,4,8,256]{4,3,2,1,0:T(8,128)(2,1)} %copy_dynamic-update-slice_fusion.40) | data formatting | bytes 9437184 | tf_op jit(solution)/shard_map/reshape | solution.py:54
  117.7 3.5 %fusion.115 = f32[8192,32]{0,1:T(8,128)S(1)} fusion(bf16[32,288]{1,0:T(8,128)(2,1)S(1)} %reshape.214, bf16[288,8192]{1,0:T(8,128)(2,1)} %reshape.213), kind=kOutput, calls=%fused_computation.301 | convolution fusion | flops 150994944 | bytes 5785600 | tf_op jit(solution)/shard_map/dot_general | solution.py:56
  121.2 3.4 %convolution_add_fusion.3 = f32[8192,32]{0,1:T(8,128)S(1)} fusion(f32[8192,32]{0,1:T(8,128)S(1)} %fusion.115, bf16[32,288]{1,0:T(8,128)(2,1)S(1)} %reshape.216, bf16[288,8192]{1,0:T(8,128)(2,1)} %reshape.215), kind=kOutput, calls=%fused_computation.5 | convolution fusion | flops 151257088 | bytes 6834176 | tf_op jit(solution)/shard_map/dot_general | solution.py:56
  125.8 3.5 %collective-permute-start.6 = (bf16[32,1,8,256]{3,2,1,0:T(8,128)(2,1)S(1)}, bf16[32,1,8,256]{3,2,1,0:T(8,128)(2,1)S(1)}, u32[]{:S(2)}, u32[]{:S(2)}) collective-permute-start(bf16[32,1,8,256]{3,2,1,0:T(8,128)(2,1)S(1)} %get-tuple-element.69), channel_id=1, source_target_pairs={{0,4},{4,8},{8,12},{1,5},{5,9},{9,13},{2,6},{6,10},{10,14},{3,7},{... | collective-permute-start | bytes 393224 | tf_op jit(solution)/shard_map/ppermute | solution.py:31
  133.1 4.9 %collective-permute-done.7 = bf16[32,1,8,256]{3,2,1,0:T(8,128)(2,1)S(1)} collective-permute-done((bf16[32,1,8,256]{3,2,1,0:T(8,128)(2,1)S(1)}, bf16[32,1,8,256]{3,2,1,0:T(8,128)(2,1)S(1)}, u32[]{:S(2)}, u32[]{:S(2)}) %collective-permute-start.7) | collective-permute-done | bytes 131104 | tf_op jit(solution)/shard_map/ppermute | solution.py:32
  138.0 3.5 %copy.175 = bf16[32,6,8,256]{0,1,3,2:T(8,128)(2,1)} copy(bf16[32,6,8,256]{3,2,1,0:T(8,128)(2,1)S(1)} %constant_dynamic-update-slice_fusion.3) | data formatting | bytes 1572864 | tf_op jit(solution)/shard_map/concatenate | solution.py:33
  146.1 9.7 %collective-permute-done.8 = bf16[32,6,1,256]{0,1,3,2:T(8,128)(2,1)S(1)} collective-permute-done((bf16[32,6,1,256]{0,1,3,2:T(8,128)(2,1)S(1)}, bf16[32,6,1,256]{0,1,3,2:T(8,128)(2,1)S(1)}, u32[]{:S(2)}, u32[]{:S(2)}) %collective-permute-start.8) | collective-permute-done | bytes 98336 | tf_op jit(solution)/shard_map/ppermute | solution.py:31
  155.8 4.1 %collective-permute-done.9 = bf16[32,6,1,256]{0,1,3,2:T(8,128)(2,1)S(1)} collective-permute-done((bf16[32,6,1,256]{0,1,3,2:T(8,128)(2,1)S(1)}, bf16[32,6,1,256]{0,1,3,2:T(8,128)(2,1)S(1)}, u32[]{:S(2)}, u32[]{:S(2)}) %collective-permute-start.9) | collective-permute-done | bytes 98336 | tf_op jit(solution)/shard_map/ppermute | solution.py:32
  159.9 4.0 %pad_maximum_fusion.1 = bf16[32,6,10,256]{0,1,3,2:T(8,128)(2,1)S(1)} fusion(bf16[32,6,1,256]{0,1,3,2:T(8,128)(2,1)S(1)} %collective-permute-done.9, bf16[32,6,8,256]{0,1,3,2:T(8,128)(2,1)} %copy.175, bf16[32,6,1,256]{0,1,3,2:T(8,128)(2,1)S(1)} %collective-permute-done.8), kind=kLoop, calls=%fused_computation.8 | loop fusion | flops 983040 | bytes 1966080 | tf_op jit(solution)/shard_map/concatenate | solution.py:33
  173.5 4.7 %copy.179 = bf16[32,6,10,256]{3,0,2,1:T(8,128)(2,1)S(1)} copy(bf16[32,6,10,256]{0,1,3,2:T(8,128)(2,1)} %copy-done.1) | data formatting | bytes 1966080 | tf_op jit(solution)/shard_map/concatenate | solution.py:33
  179.4 3.7 %fusion.85 = (bf16[1,32,4,8,256]{4,1,3,2,0:T(8,128)(2,1)}, bf16[1,32,4,8,256]{4,1,3,2,0:T(8,128)(2,1)S(1)}, bf16[1,32,4,8,256]{4,1,3,2,0:T(8,128)(2,1)}, bf16[1,...) fusion(bf16[32,6,10,256]{3,0,2,1:T(8,128)(2,1)S(1)} %copy.179, ...), kind=kLoop, calls=%fused_computation.182 | loop fusion | flops 9437184 | bytes 5705472 | tf_op jit(solution)/shard_map/stack | solution.py:46
  186.1 5.5 %fusion.83 = (bf16[1,32,4,8,256]{4,1,3,2,0:T(8,128)(2,1)S(1)}, bf16[1,32,4,8,256]{4,1,3,2,0:T(8,128)(2,1)S(1)}, bf16[1,32,4,8,256]{4,1,3,2,0:T(8,128)(2,1)}, bf1...) fusion(bf16[32,6,10,1]{3,0,2,1:T(8,128)(2,1)} %copy.183, ...), kind=kLoop, calls=%fused_computation.178 | loop fusion | flops 9437184 | bytes 5705472 | tf_op jit(solution)/shard_map/stack | solution.py:46
  205.9 8.3 %reshape.223 = bf16[288,8192]{1,0:T(8,128)(2,1)} reshape(bf16[9,32,4,8,256]{4,3,2,1,0:T(8,128)(2,1)} %copy_dynamic-update-slice_fusion) | data formatting | bytes 9437184 | tf_op jit(solution)/shard_map/reshape | solution.py:54
  228.1 8.5 %reshape.221 = bf16[288,8192]{1,0:T(8,128)(2,1)} reshape(bf16[9,32,4,8,256]{4,3,2,1,0:T(8,128)(2,1)} %copy_dynamic-update-slice_fusion.8) | data formatting | bytes 9437184 | tf_op jit(solution)/shard_map/reshape | solution.py:54
  241.0 8.3 %reshape.219 = bf16[288,8192]{1,0:T(8,128)(2,1)} reshape(bf16[9,32,4,8,256]{4,3,2,1,0:T(8,128)(2,1)} %copy_dynamic-update-slice_fusion.16) | data formatting | bytes 9437184 | tf_op jit(solution)/shard_map/reshape | solution.py:54
  249.3 3.5 %fusion.116 = f32[8192,32]{0,1:T(8,128)S(1)} fusion(bf16[32,288]{1,0:T(8,128)(2,1)S(1)} %reshape.220, bf16[288,8192]{1,0:T(8,128)(2,1)} %reshape.219), kind=kOutput, calls=%fused_computation.302 | convolution fusion | flops 150994944 | bytes 5785600 | tf_op jit(solution)/shard_map/dot_general | solution.py:56
  252.8 3.4 %convolution_add_fusion.1 = f32[8192,32]{0,1:T(8,128)S(1)} fusion(f32[8192,32]{0,1:T(8,128)S(1)} %fusion.116, bf16[32,288]{1,0:T(8,128)(2,1)S(1)} %reshape.222, bf16[288,8192]{1,0:T(8,128)(2,1)} %reshape.221), kind=kOutput, calls=%fused_computation.2 | convolution fusion | flops 151257088 | bytes 6834176 | tf_op jit(solution)/shard_map/dot_general | solution.py:56
  261.8 4.5 %collective-permute-done.12 = bf16[1,32,256]{1,2,0:T(8,128)(2,1)S(1)} collective-permute-done((bf16[1,32,256]{1,2,0:T(8,128)(2,1)S(1)}, bf16[1,32,256]{1,2,0:T(8,128)(2,1)S(1)}, u32[]{:S(2)}, u32[]{:S(2)}) %collective-permute-start.12) | collective-permute-done | bytes 16416 | tf_op jit(solution)/shard_map/ppermute | solution.py:14
  266.3 6.3 %collective-permute-done.13 = bf16[1,32,256]{1,2,0:T(8,128)(2,1)S(1)} collective-permute-done((bf16[1,32,256]{1,2,0:T(8,128)(2,1)S(1)}, bf16[1,32,256]{1,2,0:T(8,128)(2,1)S(1)}, u32[]{:S(2)}, u32[]{:S(2)}) %collective-permute-start.13) | collective-permute-done | bytes 16416 | tf_op jit(solution)/shard_map/ppermute | solution.py:14
  272.7 6.0 %collective-permute-done.14 = bf16[1,32,256]{1,2,0:T(8,128)(2,1)S(1)} collective-permute-done((bf16[1,32,256]{1,2,0:T(8,128)(2,1)S(1)}, bf16[1,32,256]{1,2,0:T(8,128)(2,1)S(1)}, u32[]{:S(2)}, u32[]{:S(2)}) %collective-permute-start.14) | collective-permute-done | bytes 16416 | tf_op jit(solution)/shard_map/ppermute | solution.py:14
  (211 shorter events, 111.8 us)
Async XLA Ops:
  1.6 8.2 %collective-permute-start = (bf16[32,1,8,256]{3,2,1,0:T(8,128)(2,1)S(1)}, bf16[32,1,8,256]{3,2,1,0:T(8,128)(2,1)S(1)}, u32[]{:S(2)}, u32[]{:S(2)}) collective-permute-start(bf16[32,1,8,256]{3,2,1,0:T(8,128)(2,1)S(1)} %get-tuple-element.74), channel_id=1, source_target_pairs={{0,4},{4,8},{8,12},{1,5},{5,9},{9,13},{2,6},{6,10},{10,14},{3,7},{... | collective-permute-start | bytes 393224 | tf_op jit(solution)/shard_map/ppermute | solution.py:31
  6.6 17.5 %copy-start.33 = (s32[1,1,1,256]{3,2,1,0:T(1,128)S(1)}, s32[1,1,1,256]{3,2,1,0:T(1,128)}, u32[]{:S(2)}) copy-start(s32[1,1,1,256]{3,2,1,0:T(1,128)} %param.9) | copy-start | bytes 3076
  6.6 6.9 %collective-permute-start.1 = (bf16[32,1,8,256]{3,2,1,0:T(8,128)(2,1)S(1)}, bf16[32,1,8,256]{3,2,1,0:T(8,128)(2,1)S(1)}, u32[]{:S(2)}, u32[]{:S(2)}) collective-permute-start(bf16[32,1,8,256]{3,2,1,0:T(8,128)(2,1)S(1)} %get-tuple-element.73), channel_id=1, source_target_pairs={{4,0},{8,4},{12,8},{5,1},{9,5},{13,9},{6,2},{10,6},{14,10},{7,3},{... | collective-permute-start | bytes 393224 | tf_op jit(solution)/shard_map/ppermute | solution.py:32
  19.3 13.4 %collective-permute-start.2 = (bf16[32,6,1,256]{0,1,3,2:T(8,128)(2,1)}, bf16[32,6,1,256]{0,1,3,2:T(8,128)(2,1)S(1)}, u32[]{:S(2)}, u32[]{:S(2)}) collective-permute-start(bf16[32,6,1,256]{0,1,3,2:T(8,128)(2,1)} %get-tuple-element.10), channel_id=1, source_target_pairs={{0,2},{1,3},{4,6},{5,7},{8,10},{9,11},{12,14},{13,15},{16,18},{17,... | collective-permute-start | bytes 294920 | tf_op jit(solution)/shard_map/ppermute | solution.py:31
  22.8 14.1 %collective-permute-start.3 = (bf16[32,6,1,256]{0,1,3,2:T(8,128)(2,1)}, bf16[32,6,1,256]{0,1,3,2:T(8,128)(2,1)S(1)}, u32[]{:S(2)}, u32[]{:S(2)}) collective-permute-start(bf16[32,6,1,256]{0,1,3,2:T(8,128)(2,1)} %get-tuple-element.11), channel_id=1, source_target_pairs={{2,0},{3,1},{6,4},{7,5},{10,8},{11,9},{14,12},{15,13},{18,16},{19,... | collective-permute-start | bytes 294920 | tf_op jit(solution)/shard_map/ppermute | solution.py:32
  43.0 9.7 %collective-permute-start.4 = (bf16[32,6,10,1]{0,1,3,2:T(8,128)(2,1)S(1)}, bf16[32,6,10,1]{0,1,3,2:T(8,128)(2,1)S(1)}, u32[]{:S(2)}, u32[]{:S(2)}) collective-permute-start(bf16[32,6,10,1]{0,1,3,2:T(8,128)(2,1)S(1)} %get-tuple-element.7), channel_id=1, source_target_pairs={{0,1},{2,3},{4,5},{6,7},{8,9},{10,11},{12,13},{14,15},{16,17},{18,... | collective-permute-start | bytes 11528 | tf_op jit(solution)/shard_map/ppermute | solution.py:31
  44.3 13.6 %collective-permute-start.5 = (bf16[32,6,10,1]{0,1,3,2:T(8,128)(2,1)S(1)}, bf16[32,6,10,1]{0,1,3,2:T(8,128)(2,1)S(1)}, u32[]{:S(2)}, u32[]{:S(2)}) collective-permute-start(bf16[32,6,10,1]{0,1,3,2:T(8,128)(2,1)S(1)} %get-tuple-element.6), channel_id=1, source_target_pairs={{1,0},{3,2},{5,4},{7,6},{9,8},{11,10},{13,12},{15,14},{17,16},{19,... | collective-permute-start | bytes 11528 | tf_op jit(solution)/shard_map/ppermute | solution.py:32
  59.1 10.7 %copy-start.12 = (bf16[1,32,4,8,256]{4,1,3,2,0:T(8,128)(2,1)S(1)}, bf16[1,32,4,8,256]{4,1,3,2,0:T(8,128)(2,1)}, u32[]{:S(2)}) copy-start(bf16[1,32,4,8,256]{4,1,3,2,0:T(8,128)(2,1)} %get-tuple-element.41) | copy-start | bytes 1572868
  59.1 11.8 %copy-start.26 = (bf16[1,32,4,8,256]{4,1,3,2,0:T(8,128)(2,1)S(1)}, bf16[1,32,4,8,256]{4,1,3,2,0:T(8,128)(2,1)}, u32[]{:S(2)}) copy-start(bf16[1,32,4,8,256]{4,1,3,2,0:T(8,128)(2,1)} %get-tuple-element.63) | copy-start | bytes 1572868
  64.2 9.9 %copy-start.25 = (bf16[1,32,4,8,256]{4,1,3,2,0:T(8,128)(2,1)S(1)}, bf16[1,32,4,8,256]{4,1,3,2,0:T(8,128)(2,1)}, u32[]{:S(2)}) copy-start(bf16[1,32,4,8,256]{4,1,3,2,0:T(8,128)(2,1)} %get-tuple-element.65) | copy-start | bytes 1572868
  65.4 11.0 %copy-start.9 = (bf16[1,32,4,8,256]{4,1,3,2,0:T(8,128)(2,1)S(1)}, bf16[1,32,4,8,256]{4,1,3,2,0:T(8,128)(2,1)}, u32[]{:S(2)}) copy-start(bf16[1,32,4,8,256]{4,1,3,2,0:T(8,128)(2,1)} %get-tuple-element.47) | copy-start | bytes 1572868
  66.5 11.0 %copy-start.2 = (bf16[32,4,8,256]{3,2,1,0:T(8,128)(2,1)S(1)}, bf16[32,4,8,256]{3,2,1,0:T(8,128)(2,1)}, u32[]{:S(2)}) copy-start(bf16[32,4,8,256]{3,2,1,0:T(8,128)(2,1)} %param.6) | copy-start | bytes 1572868
  84.6 10.5 %copy-start.5 = (bf16[1,32,4,8,256]{4,1,3,2,0:T(8,128)(2,1)S(1)}, bf16[1,32,4,8,256]{4,1,3,2,0:T(8,128)(2,1)}, u32[]{:S(2)}) copy-start(bf16[1,32,4,8,256]{4,1,3,2,0:T(8,128)(2,1)} %get-tuple-element.36) | copy-start | bytes 1572868
  96.2 11.0 %copy-start.20 = (bf16[1,32,4,8,256]{4,1,3,2,0:T(8,128)(2,1)S(1)}, bf16[1,32,4,8,256]{4,1,3,2,0:T(8,128)(2,1)}, u32[]{:S(2)}) copy-start(bf16[1,32,4,8,256]{4,1,3,2,0:T(8,128)(2,1)} %get-tuple-element.55) | copy-start | bytes 1572868
  125.8 7.2 %collective-permute-start.6 = (bf16[32,1,8,256]{3,2,1,0:T(8,128)(2,1)S(1)}, bf16[32,1,8,256]{3,2,1,0:T(8,128)(2,1)S(1)}, u32[]{:S(2)}, u32[]{:S(2)}) collective-permute-start(bf16[32,1,8,256]{3,2,1,0:T(8,128)(2,1)S(1)} %get-tuple-element.69), channel_id=1, source_target_pairs={{0,4},{4,8},{8,12},{1,5},{5,9},{9,13},{2,6},{6,10},{10,14},{3,7},{... | collective-permute-start | bytes 393224 | tf_op jit(solution)/shard_map/ppermute | solution.py:31
  129.8 8.1 %collective-permute-start.7 = (bf16[32,1,8,256]{3,2,1,0:T(8,128)(2,1)S(1)}, bf16[32,1,8,256]{3,2,1,0:T(8,128)(2,1)S(1)}, u32[]{:S(2)}, u32[]{:S(2)}) collective-permute-start(bf16[32,1,8,256]{3,2,1,0:T(8,128)(2,1)S(1)} %get-tuple-element.68), channel_id=1, source_target_pairs={{4,0},{8,4},{12,8},{5,1},{9,5},{13,9},{6,2},{10,6},{14,10},{7,3},{... | collective-permute-start | bytes 393224 | tf_op jit(solution)/shard_map/ppermute | solution.py:32
  138.0 26.0 %copy-start.28 = (bf16[32,1,8,256]{3,2,1,0:T(8,128)(2,1)}, bf16[32,1,8,256]{3,2,1,0:T(8,128)(2,1)S(1)}, u32[]{:S(2)}) copy-start(bf16[32,1,8,256]{3,2,1,0:T(8,128)(2,1)S(1)} %collective-permute-done.7) | copy-start | bytes 393220
  142.9 12.9 %collective-permute-start.8 = (bf16[32,6,1,256]{0,1,3,2:T(8,128)(2,1)S(1)}, bf16[32,6,1,256]{0,1,3,2:T(8,128)(2,1)S(1)}, u32[]{:S(2)}, u32[]{:S(2)}) collective-permute-start(bf16[32,6,1,256]{0,1,3,2:T(8,128)(2,1)S(1)} %get-tuple-element.8), channel_id=1, source_target_pairs={{0,2},{1,3},{4,6},{5,7},{8,10},{9,11},{12,14},{13,15},{16,18},{17,... | collective-permute-start | bytes 294920 | tf_op jit(solution)/shard_map/ppermute | solution.py:31
  144.5 15.4 %collective-permute-start.9 = (bf16[32,6,1,256]{0,1,3,2:T(8,128)(2,1)S(1)}, bf16[32,6,1,256]{0,1,3,2:T(8,128)(2,1)S(1)}, u32[]{:S(2)}, u32[]{:S(2)}) collective-permute-start(bf16[32,6,1,256]{0,1,3,2:T(8,128)(2,1)S(1)} %get-tuple-element.9), channel_id=1, source_target_pairs={{2,0},{3,1},{6,4},{7,5},{10,8},{11,9},{14,12},{15,13},{18,16},{19,... | collective-permute-start | bytes 294920 | tf_op jit(solution)/shard_map/ppermute | solution.py:32
  167.0 11.2 %collective-permute-start.10 = (bf16[32,6,10,1]{0,1,3,2:T(8,128)(2,1)}, bf16[32,6,10,1]{0,1,3,2:T(8,128)(2,1)}, u32[]{:S(2)}, u32[]{:S(2)}) collective-permute-start(bf16[32,6,10,1]{0,1,3,2:T(8,128)(2,1)} %get-tuple-element.5), channel_id=1, source_target_pairs={{0,1},{2,3},{4,5},{6,7},{8,9},{10,11},{12,13},{14,15},{16,17},{18,... | collective-permute-start | bytes 11528 | tf_op jit(solution)/shard_map/ppermute | solution.py:31
  168.8 15.3 %collective-permute-start.11 = (bf16[32,6,10,1]{0,1,3,2:T(8,128)(2,1)}, bf16[32,6,10,1]{0,1,3,2:T(8,128)(2,1)}, u32[]{:S(2)}, u32[]{:S(2)}) collective-permute-start(bf16[32,6,10,1]{0,1,3,2:T(8,128)(2,1)} %get-tuple-element.4), channel_id=1, source_target_pairs={{1,0},{3,2},{5,4},{7,6},{9,8},{11,10},{13,12},{15,14},{17,16},{19,... | collective-permute-start | bytes 11528 | tf_op jit(solution)/shard_map/ppermute | solution.py:32
  186.1 10.9 %copy-start.27 = (bf16[1,32,4,8,256]{4,1,3,2,0:T(8,128)(2,1)S(1)}, bf16[1,32,4,8,256]{4,1,3,2,0:T(8,128)(2,1)}, u32[]{:S(2)}) copy-start(bf16[1,32,4,8,256]{4,1,3,2,0:T(8,128)(2,1)} %get-tuple-element.62) | copy-start | bytes 1572868
  186.1 13.1 %copy-start.11 = (bf16[1,32,4,8,256]{4,1,3,2,0:T(8,128)(2,1)S(1)}, bf16[1,32,4,8,256]{4,1,3,2,0:T(8,128)(2,1)}, u32[]{:S(2)}) copy-start(bf16[1,32,4,8,256]{4,1,3,2,0:T(8,128)(2,1)} %get-tuple-element.29) | copy-start | bytes 1572868
  192.7 9.9 %copy-start.8 = (bf16[1,32,4,8,256]{4,1,3,2,0:T(8,128)(2,1)S(1)}, bf16[1,32,4,8,256]{4,1,3,2,0:T(8,128)(2,1)}, u32[]{:S(2)}) copy-start(bf16[1,32,4,8,256]{4,1,3,2,0:T(8,128)(2,1)} %get-tuple-element.21) | copy-start | bytes 1572868
  214.2 10.6 %copy-start.3 = (bf16[1,32,4,8,256]{4,1,3,2,0:T(8,128)(2,1)S(1)}, bf16[1,32,4,8,256]{4,1,3,2,0:T(8,128)(2,1)}, u32[]{:S(2)}) copy-start(bf16[1,32,4,8,256]{4,1,3,2,0:T(8,128)(2,1)} %get-tuple-element.27) | copy-start | bytes 1572868
  214.2 11.7 %copy-start.22 = (bf16[1,32,4,8,256]{4,1,3,2,0:T(8,128)(2,1)S(1)}, bf16[1,32,4,8,256]{4,1,3,2,0:T(8,128)(2,1)}, u32[]{:S(2)}) copy-start(bf16[1,32,4,8,256]{4,1,3,2,0:T(8,128)(2,1)} %get-tuple-element.50) | copy-start | bytes 1572868
  214.2 12.8 %copy-start.6 = (bf16[1,32,4,8,256]{4,1,3,2,0:T(8,128)(2,1)S(1)}, bf16[1,32,4,8,256]{4,1,3,2,0:T(8,128)(2,1)}, u32[]{:S(2)}) copy-start(bf16[1,32,4,8,256]{4,1,3,2,0:T(8,128)(2,1)} %get-tuple-element.18) | copy-start | bytes 1572868
  228.1 10.8 %copy-start.21 = (bf16[1,32,4,8,256]{4,1,3,2,0:T(8,128)(2,1)S(1)}, bf16[1,32,4,8,256]{4,1,3,2,0:T(8,128)(2,1)}, u32[]{:S(2)}) copy-start(bf16[1,32,4,8,256]{4,1,3,2,0:T(8,128)(2,1)} %get-tuple-element.49) | copy-start | bytes 1572868
  257.8 23.1 %copy-start.17 = (bf16[32,4,8,256]{3,2,1,0:T(8,128)(2,1)}, bf16[32,4,8,256]{3,2,1,0:T(8,128)(2,1)S(1)}, u32[]{:S(2)}) copy-start(bf16[32,4,8,256]{3,2,1,0:T(8,128)(2,1)S(1)} %add_convert_fusion) | copy-start | bytes 1572868
  260.2 6.1 %collective-permute-start.12 = (bf16[1,32,256]{1,2,0:T(8,128)(2,1)S(1)}, bf16[1,32,256]{1,2,0:T(8,128)(2,1)S(1)}, u32[]{:S(2)}, u32[]{:S(2)}) collective-permute-start(bf16[1,32,256]{1,2,0:T(8,128)(2,1)S(1)} %divide_convert_fusion), channel_id=1, source_target_pairs={{0,4},{4,8},{8,12},{12,0},{1,5},{5,9},{9,13},{13,1},{2,6},{6,10},{... | collective-permute-start | bytes 49160 | tf_op jit(solution)/shard_map/ppermute | solution.py:14
  266.3 6.4 %collective-permute-start.13 = (bf16[1,32,256]{1,2,0:T(8,128)(2,1)S(1)}, bf16[1,32,256]{1,2,0:T(8,128)(2,1)S(1)}, u32[]{:S(2)}, u32[]{:S(2)}) collective-permute-start(bf16[1,32,256]{1,2,0:T(8,128)(2,1)S(1)} %collective-permute-done.12), channel_id=1, source_target_pairs={{0,4},{4,8},{8,12},{12,0},{1,5},{5,9},{9,13},{13,1},{2,6},{6,10},{... | collective-permute-start | bytes 49160 | tf_op jit(solution)/shard_map/ppermute | solution.py:14
  272.6 6.1 %collective-permute-start.14 = (bf16[1,32,256]{1,2,0:T(8,128)(2,1)S(1)}, bf16[1,32,256]{1,2,0:T(8,128)(2,1)S(1)}, u32[]{:S(2)}, u32[]{:S(2)}) collective-permute-start(bf16[1,32,256]{1,2,0:T(8,128)(2,1)S(1)} %collective-permute-done.13), channel_id=1, source_target_pairs={{0,4},{4,8},{8,12},{12,0},{1,5},{5,9},{9,13},{13,1},{2,6},{6,10},{... | collective-permute-start | bytes 49160 | tf_op jit(solution)/shard_map/ppermute | solution.py:14
  (21 other events, 141.2 us)
